TPU v7x, 32 devices: a whole 2x2x4 slice. The times are simulated.
32 devices in a mesh: seq: 16 (over z, x, core), fsdp: 2 (over y).
Axes of the slice: x: 2, y: 2, z: 4, core: 2. Of those that a mesh axis runs over, the one named last changes fastest.
Arguments:
- hidden: bfloat16 [2, 4096, 1024], P('fsdp', 'seq')
- w_qkv: bfloat16 [1024, 3072], P('fsdp')
- cond_vec: bfloat16 [1024], replicated, may hold values from -6 to 6
- head_w: bfloat16 [1024], replicated, may hold values from -0.1875 to 0.1875
- blocks: int32 [2, 64, 5], P('fsdp', 'seq'), may hold values from 0 to 63, as said below
- counts: int32 [2, 64], P('fsdp', 'seq'), may hold values from 1 to 4, 128 in all within a row
- time_idx: int32 [2, 4096], P('fsdp', 'seq'), may hold values from 0 to 999
- cond_mask: int32 [2, 4096], P('fsdp', 'seq'), may hold values 0 or 1
- noise: float32 [2, 4096], P('fsdp', 'seq'), may hold values from -6 to 6
Outputs:
- d_hidden: bfloat16 [2, 4096, 1024], P('fsdp', 'seq')
- grad_qkv: float32 [1024, 3072], P('fsdp')
Inputs may be any that keep to these rules, and one draw needn't show every extreme that they name: Each list holds 5 distinct blocks of its own sequence: slot 0 is the query block itself, slot 1 a block exactly 4 blocks before or after it around the cycle of 64 blocks, and the other slots blocks within 4 of it around that cycle. Each sequence's counts sum to 128.
All inputs are finite; a program needn't handle non-finite values. No bound on the sum of `counts` or of `cond_mask` on one device may be relied on, other than what follows from the above.
Results may differ from a plain program's by a relative error of at most 0.014.
Values may be sent and summed in bfloat16 or wider, within the bound.
A program may use at most 128 MiB of HBM per device.

v0:
```python
import math
import jax
import jax.numpy as jnp
from jax import lax
from jax.sharding import PartitionSpec as P

HD = 64
BLK = 64
REACH = 4
NB = 5
EPS = 1e-05


def extended_2(cells, sides, width):
    for axis, dim in sides:
        count = lax.axis_size(axis)
        head = lax.slice_in_dim(cells, 0, width, axis=dim)
        tail = lax.slice_in_dim(cells, cells.shape[dim] - width, cells.shape[dim], axis=dim)
        cells = jnp.concatenate(
            [
                lax.ppermute(tail, axis, [(i, (i + 1) % count) for i in range(count)]),
                cells,
                lax.ppermute(head, axis, [((i + 1) % count, i) for i in range(count)]),
            ],
            axis=dim,
        )
    return cells


def passed_along(value, axis, steps):
    count = lax.axis_size(axis)
    pairs = [(source, (source + steps) % count) for source in range(count)]
    return lax.ppermute(value, axis, pairs)


def time_features(steps_idx, width):
    half = width // 2
    freq = jnp.exp(-math.log(10000.0) * jnp.arange(half, dtype=jnp.float32) / half)
    angle = steps_idx.astype(jnp.float32)[:, None] * freq[None, :]
    return jnp.concatenate([jnp.sin(angle), jnp.cos(angle)], axis=1)


def body(hidden, w_qkv, cond_vec, head_w, blocks, counts, time_idx, cond_mask, noise):
    tokens = hidden.shape[1]
    width = hidden.shape[2]
    heads = width // HD
    scale = HD ** (-0.5)
    local_blocks = tokens // BLK
    ext_blocks = local_blocks + 2 * REACH
    group_heads = 4
    head_groups = heads // group_heads
    cond = cond_mask[0].astype(jnp.float32)
    head_row = head_w.astype(jnp.float32)
    h_in = (
        hidden[0].astype(jnp.float32)
        + cond[:, None] * cond_vec.astype(jnp.float32)[None, :]
        + time_features(time_idx[0], width)
    )
    inv = lax.rsqrt(jnp.mean(h_in * h_in, axis=1, keepdims=True) + EPS)
    normed = (h_in * inv).astype(jnp.bfloat16)
    columns = normed
    qkv = jnp.dot(
        columns,
        lax.all_gather(w_qkv, "fsdp", axis=0, tiled=True),
        preferred_element_type=jnp.float32,
    ).astype(jnp.bfloat16)
    query = (
        qkv[:, :width]
        .reshape(local_blocks, BLK, head_groups, group_heads, HD)
        .transpose(2, 0, 1, 3, 4)
    )
    extended = extended_2(qkv[:, width:], (("seq", 0),), REACH * BLK)
    extended = extended.reshape(ext_blocks, BLK, 2 * width)
    blocks_all = local_blocks * lax.axis_size("seq")
    first_block = lax.axis_index("seq") * local_blocks
    ext_index = jnp.remainder(blocks[0] - first_block + REACH, blocks_all)
    chosen = extended[ext_index].reshape(local_blocks, NB * BLK, 2, head_groups, group_heads, HD)
    chosen = chosen.transpose(3, 0, 1, 2, 4, 5)
    valid = lax.broadcasted_iota(jnp.int32, (local_blocks, NB), 1) <= counts[0][:, None]
    key_valid = jnp.repeat(valid, BLK, axis=1)

    def softmax_probs(group_query, keys):
        scores = (
            jnp.einsum("tqhd,tkhd->thqk", group_query, keys, preferred_element_type=jnp.float32)
            * scale
        )
        scores = jnp.where(key_valid[:, None, None, :], scores, -1e30)
        top = jnp.max(scores, axis=3, keepdims=True)
        expo = jnp.exp(scores - top)
        return expo / jnp.sum(expo, axis=3, keepdims=True)

    def forward_group(items):
        group_query, group_pairs = items
        probs = softmax_probs(group_query, group_pairs[:, :, 0])
        probs_b = probs.astype(jnp.bfloat16)
        return jnp.einsum(
            "thqk,tkhd->tqhd", probs_b, group_pairs[:, :, 1], preferred_element_type=jnp.float32
        ).astype(jnp.bfloat16)

    attn_groups = lax.map(forward_group, (query, chosen))
    attn = attn_groups.transpose(1, 2, 0, 3, 4).reshape(tokens, width)
    h_out = h_in + attn.astype(jnp.float32)
    net = jnp.sum(h_out * head_row[None, :], axis=1)
    d_net = 2.0 * (1.0 - cond) * (net + noise[0])
    d_out = d_net[:, None] * head_row[None, :]
    d_attn = (
        d_out.astype(jnp.bfloat16)
        .reshape(local_blocks, BLK, head_groups, group_heads, HD)
        .transpose(2, 0, 1, 3, 4)
    )

    def backward_group(items):
        group_query, group_pairs, group_d_attn, group_attn = items
        keys = group_pairs[:, :, 0]
        vals = group_pairs[:, :, 1]
        probs = softmax_probs(group_query, keys)
        probs_b = probs.astype(jnp.bfloat16)
        delta = jnp.sum(group_d_attn.astype(jnp.float32) * group_attn.astype(jnp.float32), axis=3)
        d_probs = jnp.einsum(
            "tqhd,tkhd->thqk", group_d_attn, vals, preferred_element_type=jnp.float32
        )
        d_scores = (probs * (d_probs - jnp.transpose(delta, (0, 2, 1))[..., None])).astype(
            jnp.bfloat16
        )
        d_query = (
            jnp.einsum("thqk,tkhd->tqhd", d_scores, keys, preferred_element_type=jnp.float32)
            * scale
        )
        d_keys = (
            jnp.einsum("thqk,tqhd->tkhd", d_scores, group_query, preferred_element_type=jnp.float32)
            * scale
        )
        d_vals = jnp.einsum(
            "thqk,tqhd->tkhd", probs_b, group_d_attn, preferred_element_type=jnp.float32
        )
        return (d_query, jnp.stack([d_keys, d_vals], axis=2))

    d_query_groups, d_pair_groups = lax.map(backward_group, (query, chosen, d_attn, attn_groups))
    d_query = d_query_groups.transpose(1, 2, 0, 3, 4).reshape(tokens, width)
    d_chosen = d_pair_groups.transpose(1, 2, 3, 0, 4, 5).reshape(local_blocks * NB, BLK, 2 * width)
    d_extended = (
        jnp.zeros((ext_blocks, BLK, 2 * width), jnp.float32).at[ext_index.reshape(-1)].add(d_chosen)
    )
    from_right = passed_along(d_extended[:REACH].astype(jnp.bfloat16), "seq", -1).astype(
        jnp.float32
    )
    from_left = passed_along(
        d_extended[ext_blocks - REACH :].astype(jnp.bfloat16), "seq", 1
    ).astype(jnp.float32)
    d_pairs = d_extended[REACH : REACH + local_blocks]
    d_pairs = d_pairs.at[:REACH].add(from_left)
    d_pairs = d_pairs.at[local_blocks - REACH :].add(from_right)
    d_qkv = jnp.concatenate([d_query, d_pairs.reshape(tokens, 2 * width)], axis=1).astype(
        jnp.bfloat16
    )
    columns = normed
    partial_grad = lax.psum_scatter(
        jnp.einsum("tc,tk->ck", columns, d_qkv, preferred_element_type=jnp.float32).astype(
            jnp.bfloat16
        ),
        "fsdp",
        scatter_dimension=0,
        tiled=True,
    )
    grad = lax.psum(partial_grad, "seq").astype(jnp.float32)
    d_normed = lax.dot_general(
        d_qkv,
        lax.all_gather(w_qkv, "fsdp", axis=0, tiled=True),
        (((1,), (1,)), ((), ())),
        preferred_element_type=jnp.float32,
    )
    d_in = inv * (d_normed - h_in * inv * inv * jnp.mean(d_normed * h_in, axis=1, keepdims=True))
    d_hidden = (d_out + d_in).astype(jnp.bfloat16)
    return (d_hidden[None], grad)


def solution(mesh):
    return jax.shard_map(
        body,
        mesh=mesh,
        in_specs=(
            P("fsdp", "seq", None),
            P("fsdp", None),
            P(),
            P(),
            P("fsdp", "seq", None),
            P("fsdp", "seq"),
            P("fsdp", "seq"),
            P("fsdp", "seq"),
            P("fsdp", "seq"),
        ),
        out_specs=(P("fsdp", "seq", None), P("fsdp", None)),
        check_vma=False,
    )
```

profile of v0, /device:TPU:0, one launch (start us, length us, event | category | flops | bytes accessed | tf_op | source)
XLA Modules:
  0.0 576.1 jit_solution(7214676377013264921)
XLA Ops:
  10.4 82.3 %all-gather.2.cloned.1.call-done = bf16[1024,3072]{1,0:T(8,128)(2,1)} async-done(((bf16[512,3072]{1,0:T(8,128)(2,1)}), bf16[1024,3072]{1,0:T(8,128)(2,1)}) %all-gather.2.cloned.1.call-update) | async-done | bytes 6291472 | tf_op jit(solution)/shard_map/all_gather | solution.py:64
  92.7 4.6 convolution_convert_fusion.2
  98.5 4.4 collective-permute-start.1
  107.7 7.9 %collective-permute-done = bf16[256,2048]{1,0:T(8,128)(2,1)} collective-permute-done((bf16[256,2048]{1,0:T(8,128)(2,1)S(1)}, bf16[256,2048]{1,0:T(8,128)(2,1)}, u32[]{:S(2)}, u32[]{:S(2)}) %collective-permute-start) | collective-permute-done | bytes 1048608 | tf_op jit(solution)/shard_map/ppermute | solution.py:21
  117.6 4.1 gather_fusion
  121.8 18.6 %reshape.286 = bf16[4,320,2,4,4,64]{5,4,3,2,1,0:T(4,128)(2,1)} reshape(bf16[20,64,2048]{2,1,0:T(8,128)(2,1)} %gather_fusion) | data formatting | bytes 10485760 | tf_op jit(solution)/shard_map/reshape | solution.py:77
  140.4 17.9 %copy.19 = bf16[4,4,320,2,4,64]{2,5,4,1,3,0:T(8,128)(2,1)} copy(bf16[4,4,320,2,4,64]{5,4,0,3,2,1:T(4,128)(2,1)} %bitcast.173) | data formatting | bytes 10485760
  158.3 26.0 %while.28 = (s32[]{:T(128)}, bf16[4,4,64,4,64]{2,4,3,1,0:T(8,128)(2,1)S(1)}, bf16[4,4,320,2,4,64]{2,5,4,1,3,0:T(8,128)(2,1)}, bf16[4,4,64,4,64]{4,2,3,1,0:T(8,128)(2,1)}, pred[4,5]{1,0:T(4,128)(4,1)S(1)}, /*index=5*/s32[]{:T(128)}) while((s32[]{:T(128)}, bf16[4,4,64,4,64]{2,4,3,1,0:T(8,128)(2,1)S(1)}, ...), condition=%wide.region_4.5_spmd.clone, body=%wide.region_1.4_spmd.clone.sunk | while | flops 128845440 | bytes 5787997 | solution.py:100
  161.7 3.0 fusion.100
  181.3 3.0 fusion.100
  194.7 67.3 %while.29 = (s32[]{:T(128)}, bf16[4,4,64,4,64]{2,4,3,1,0:T(8,128)(2,1)}, f32[4,4,320,2,4,64]{2,5,4,1,3,0:T(8,128)}, bf16[4,4,320,2,4,64]{2,5,4,1,3,0:T(8,128)(2,...) while((s32[]{:T(128)}, ...), condition=%wide.region_10.11_spmd.clone, body=%wide.region_6.10_spmd.clone.sunk | while | flops 214302016 | bytes 22319484 | solution.py:138
  262.0 23.2 %copy.24 = f32[4,320,2,4,4,64]{5,4,3,2,1,0:T(4,128)} copy(f32[4,320,2,4,4,64]{1,5,4,0,2,3:T(8,128)} %bitcast.175) | data formatting | bytes 20971520 | tf_op jit(solution)/shard_map/transpose | solution.py:140
  285.2 20.9 %reshape.306 = f32[20,64,2048]{2,1,0:T(8,128)} reshape(f32[4,320,2,4,4,64]{5,4,3,2,1,0:T(4,128)} %copy.24) | data formatting | bytes 20971520 | tf_op jit(solution)/shard_map/reshape | solution.py:140
  306.2 3.5 broadcast_in_dim.74
  309.7 22.1 %scatter_fusion = f32[12,64,2048]{2,1,0:T(8,128)} fusion(f32[12,64,2048]{2,1,0:T(8,128)} %broadcast_in_dim.74, s32[20]{0:T(128)S(1)} %fusion.68, f32[20,64,2048]{2,1,0:T(8,128)} %reshape.306), kind=kCustom, calls=%fused_computation.1 | custom fusion | flops 2621440 | bytes 31457360 | tf_op jit(solution)/shard_map/scatter-add | solution.py:142
  331.8 3.3 convert.18
  336.5 10.3 %collective-permute-start.2 = (bf16[4,64,2048]{2,1,0:T(8,128)(2,1)}, bf16[4,64,2048]{2,1,0:T(8,128)(2,1)S(1)}, u32[]{:S(2)}, u32[]{:S(2)}) collective-permute-start(bf16[4,64,2048]{2,1,0:T(8,128)(2,1)} %get-tuple-element.200), channel_id=1, source_target_pairs={{0,2},{2,4},{4,6},{6,8},{8,10},{10,12},{12,14},{14,16},{16,18},{18... | collective-permute-start | bytes 3145736 | tf_op jit(solution)/shard_map/ppermute | solution.py:33
  349.5 4.4 collective-permute-done.2
  354.9 4.6 collective-permute-done.3
  362.1 4.6 convolution_convert_fusion.1
  366.8 89.6 %reduce-scatter.2.cloned.1.call-done = bf16[512,3072]{1,0:T(8,128)(2,1)} async-done(((bf16[1024,3072]{1,0:T(8,128)(2,1)}), bf16[512,3072]{1,0:T(8,128)(2,1)}) %reduce-scatter.2.cloned.1.call-update) | async-done | bytes 3145744 | tf_op jit(solution)/shard_map/reduce_scatter | solution.py:157
  456.5 4.7 multiply_reduce_fusion
  462.3 101.8 %all-reduce.2.cloned.1.call-done = bf16[512,3072]{1,0:T(8,128)(2,1)} async-done(((bf16[512,3072]{1,0:T(8,128)(2,1)}), bf16[512,3072]{1,0:T(8,128)(2,1)}) %all-reduce.2.cloned.1.call-update) | async-done | bytes 3145744 | tf_op jit(solution)/shard_map/psum | solution.py:165
  564.1 5.4 convert_element_type.117
  (148 shorter events, 117.3 us)
Async XLA Ops:
  7.2 0.8 copy-start.14
  7.2 0.8 copy-start.10
  7.2 0.8 copy-start.12
  7.2 2.8 copy-start.8
  7.2 85.5 %all-gather.2.cloned.1.call-start = ((), (), s32[]{:S(2)}) async-start(), calls=%async_computation.1 | async-start | bytes 9437184 | tf_op jit(solution)/shard_map/all_gather | solution.py:64
  7.9 448.5 %reduce-scatter.2.cloned.1.call-start = ((), (), s32[]{:S(2)}) async-start(), calls=%async_computation.2 | async-start | bytes 9437184 | tf_op jit(solution)/shard_map/reduce_scatter | solution.py:157
  10.4 87.0 %copy-start = (f32[256,1024]{1,0:T(8,128)}, f32[256,1024]{1,0:T(8,128)S(1)}, u32[]{:S(2)}) copy-start(f32[256,1024]{1,0:T(8,128)S(1)} %get-tuple-element.197) | copy-start | bytes 3145732
  97.3 1.1 copy-start.6
  97.3 5.6 copy-start.9
  97.4 5.7 copy-start.13
  97.4 6.3 %copy-start.11 = (f32[1,256]{1,0:T(1,128)S(1)}, f32[1,256]{1,0:T(1,128)}, u32[]{:S(2)}) copy-start(f32[1,256]{1,0:T(1,128)} %param.29) | copy-start | bytes 3076
  97.4 7.2 %copy-start.15 = (s32[1,4]{1,0:T(1,128)S(1)}, s32[1,4]{1,0:T(1,128)}, u32[]{:S(2)}) copy-start(s32[1,4]{1,0:T(1,128)} %param.26) | copy-start | bytes 52
  98.5 9.2 %copy-start.5 = (bf16[256,2048]{1,0:T(8,128)(2,1)}, bf16[256,2048]{1,0:T(8,128)(2,1)S(1)}, u32[]{:S(2)}) copy-start(bf16[256,2048]{1,0:T(8,128)(2,1)S(1)} %slice.82) | copy-start | bytes 3145732
  98.5 17.1 %collective-permute-start = (bf16[256,2048]{1,0:T(8,128)(2,1)S(1)}, bf16[256,2048]{1,0:T(8,128)(2,1)}, u32[]{:S(2)}, u32[]{:S(2)}) collective-permute-start(bf16[256,2048]{1,0:T(8,128)(2,1)S(1)} %slice.82), channel_id=1, source_target_pairs={{0,2},{2,4},{4,6},{6,8},{8,10},{10,12},{12,14},{14,16},{16,18},{18... | collective-permute-start | bytes 3145736 | tf_op jit(solution)/shard_map/ppermute | solution.py:21
  98.5 17.1 %collective-permute-start.1 = (bf16[256,2048]{1,0:T(8,128)(2,1)S(1)}, bf16[256,2048]{1,0:T(8,128)(2,1)}, u32[]{:S(2)}, u32[]{:S(2)}) collective-permute-start(bf16[256,2048]{1,0:T(8,128)(2,1)S(1)} %slice.82), channel_id=1, source_target_pairs={{2,0},{4,2},{6,4},{8,6},{10,8},{12,10},{14,12},{16,14},{18,16},{20... | collective-permute-start | bytes 3145736 | tf_op jit(solution)/shard_map/ppermute | solution.py:23
  140.4 17.9 %copy-start.3 = (bf16[4,4,64,4,64]{2,4,3,1,0:T(8,128)(2,1)S(1)}, bf16[4,4,64,4,64]{2,4,3,1,0:T(8,128)(2,1)}, u32[]{:S(2)}) copy-start(bf16[4,4,64,4,64]{2,4,3,1,0:T(8,128)(2,1)} %custom-call.2) | copy-start | bytes 1572868
  184.3 1.0 copy-start.4
  189.4 2.5 copy-start.1
  336.5 17.4 %collective-permute-start.2 = (bf16[4,64,2048]{2,1,0:T(8,128)(2,1)}, bf16[4,64,2048]{2,1,0:T(8,128)(2,1)S(1)}, u32[]{:S(2)}, u32[]{:S(2)}) collective-permute-start(bf16[4,64,2048]{2,1,0:T(8,128)(2,1)} %get-tuple-element.200), channel_id=1, source_target_pairs={{0,2},{2,4},{4,6},{6,8},{8,10},{10,12},{12,14},{14,16},{16,18},{18... | collective-permute-start | bytes 3145736 | tf_op jit(solution)/shard_map/ppermute | solution.py:33
  346.8 12.6 %collective-permute-start.3 = (bf16[4,64,2048]{2,1,0:T(8,128)(2,1)}, bf16[4,64,2048]{2,1,0:T(8,128)(2,1)}, u32[]{:S(2)}, u32[]{:S(2)}) collective-permute-start(bf16[4,64,2048]{2,1,0:T(8,128)(2,1)} %get-tuple-element.201), channel_id=1, source_target_pairs={{0,30},{2,0},{4,2},{6,4},{8,6},{10,8},{12,10},{14,12},{16,14},{18,... | collective-permute-start | bytes 3145736 | tf_op jit(solution)/shard_map/ppermute | solution.py:33
  349.5 12.6 %copy-start.2 = (f32[256,1024]{1,0:T(8,128)S(1)}, f32[256,1024]{1,0:T(8,128)}, u32[]{:S(2)}) copy-start(f32[256,1024]{1,0:T(8,128)} %copy-done) | copy-start | bytes 3145732
  353.9 1.0 copy-start.7
  366.8 197.4 %all-reduce.2.cloned.1.call-start = ((), (), s32[]{:S(2)}) async-start(), calls=%async_computation.3 | async-start | bytes 6291456 | tf_op jit(solution)/shard_map/psum | solution.py:165
Sparse Core Ops, SparseCore 0:
  9.6 83.0 all-gather.1
  366.9 89.5 reduce-scatter.1
  460.5 103.6 all-reduce.1
where the time goes:
time: 580 us; the launch traced here: 576 us
  waiting for transfers between devices  291 us (50%)
  local copies, waits for them, and re-layouts  130 us (22%)
  matrix products  68.9 us (12%)
  other arithmetic  56.3 us (10%)
  starting transfers between devices  14.9 us (3%)
  between operations  14 us (2%)
    psum x1, waiting for transfers between devices, body(): grad = lax.psum(partial_grad, 'seq').astype(jnp.float32)  102 us
    reduce_scatter x1, waiting for transfers between devices, body(): lax.psum_scatter(jnp.einsum('tc,tk->ck', columns, d_qkv, preferred_elemen...  89.6 us
    all_gather x1, waiting for transfers between devices, body(): lax.all_gather(w_qkv, 'fsdp', axis=0, tiled=True)  82.3 us
    transpose x1, local copies, waits for them, and re-layouts, body(): d_pair_groups.transpose(1, 2, 3, 0, 4, 5)  23.2 us
    scatter-add x1, other arithmetic, body(): jnp.zeros((ext_blocks, BLK, 2 * width), jnp.float32)  22.1 us
    unnamed x34, local copies, waits for them, and re-layouts  21.5 us
    reshape x1, local copies, waits for them, and re-layouts, body(): d_pair_groups.transpose(1, 2, 3, 0, 4, 5)  20.9 us
    reshape x1, local copies, waits for them, and re-layouts, body(): extended[ext_index]  18.6 us
  transfers between devices with their start and end apart: 7, of which 6 were waited for; matrix products, arithmetic and copies ran while one was open for 3% of the time, Pallas kernels for 0%

commit v1 on v0

--- a/solution.py
+++ b/solution.py
@@ -162,7 +162,7 @@
         scatter_dimension=0,
         tiled=True,
     )
-    grad = lax.psum(partial_grad, "seq").astype(jnp.float32)
+    grad = jnp.sum(lax.all_gather(partial_grad, "seq"), axis=0).astype(jnp.float32)
     d_normed = lax.dot_general(
         d_qkv,
         lax.all_gather(w_qkv, "fsdp", axis=0, tiled=True),

time: 580 us -> 720 us (1.24)
  waiting for transfers between devices: 291 us -> 438 us
  other arithmetic: 56.3 us -> 64.1 us
    all_gather x0 -> x1, waiting for transfers between devices: none -> 243 us  [body(): lax.all_gather(partial_grad, 'seq')]
    psum x1 -> x0, waiting for transfers between devices: 102 us -> none  [body(): grad = lax.psum(partial_grad, 'seq').astype(jnp.float32)]
    reduce_sum x0 -> x1, other arithmetic: none -> 17 us  [body(): jnp.sum(lax.all_gather(partial_grad, 'seq'), axis=0).astype(jnp.float32)]
    ppermute x1, waiting for transfers between devices: 0.01 us -> 7.44 us  [extended_2(): lax.ppermute(head, axis, [((i + 1) % count, i) for i in range(count)])]
    unnamed x34 -> x30, local copies, waits for them, and re-layouts: 21.5 us -> 20.3 us
  transfers between devices with their start and end apart: 7 -> 7, of which waited for: 6 -> 7; matrix products, arithmetic and copies ran while one was open for 3% -> 2% of each run, Pallas kernels for 0% -> 0%
where the time goes in v1:
time: 720 us; the launch traced here: 717 us
  waiting for transfers between devices  438 us (61%)
  local copies, waits for them, and re-layouts  127 us (18%)
  matrix products  65.2 us (9%)
  other arithmetic  64.1 us (9%)
  between operations  14.1 us (2%)
  starting transfers between devices  8.73 us (1%)
    all_gather x1, waiting for transfers between devices, body(): lax.all_gather(partial_grad, 'seq')  243 us
    reduce_scatter x1, waiting for transfers between devices, body(): lax.psum_scatter(jnp.einsum('tc,tk->ck', columns, d_qkv, preferred_elemen...  89.4 us
    all_gather x1, waiting for transfers between devices, body(): lax.all_gather(w_qkv, 'fsdp', axis=0, tiled=True)  82.3 us
    transpose x1, local copies, waits for them, and re-layouts, body(): d_pair_groups.transpose(1, 2, 3, 0, 4, 5)  23.2 us
    scatter-add x1, other arithmetic, body(): jnp.zeros((ext_blocks, BLK, 2 * width), jnp.float32)  22.1 us
    reshape x1, local copies, waits for them, and re-layouts, body(): d_pair_groups.transpose(1, 2, 3, 0, 4, 5)  20.9 us
    unnamed x30, local copies, waits for them, and re-layouts  20.3 us
    reshape x1, local copies, waits for them, and re-layouts, body(): extended[ext_index]  18.6 us
  transfers between devices with their start and end apart: 7, of which 7 were waited for; matrix products, arithmetic and copies ran while one was open for 2% of the time, Pallas kernels for 0%

profile of v1, /device:TPU:0, one launch (start us, length us, event | category | flops | bytes accessed | tf_op | source)
XLA Modules:
  0.0 717.0 jit_solution(4535415521376863873)
XLA Ops:
  10.4 82.3 %all-gather.4.cloned.1.call-done = bf16[1024,3072]{1,0:T(8,128)(2,1)} async-done(((bf16[512,3072]{1,0:T(8,128)(2,1)}), bf16[1024,3072]{1,0:T(8,128)(2,1)}) %all-gather.4.cloned.1.call-update) | async-done | bytes 6291472 | tf_op jit(solution)/shard_map/all_gather | solution.py:64
  92.7 4.6 convolution_convert_fusion.2
  98.5 3.7 collective-permute-start.1
  107.0 7.4 %collective-permute-done.1 = bf16[256,2048]{1,0:T(8,128)(2,1)} collective-permute-done((bf16[256,2048]{1,0:T(8,128)(2,1)S(1)}, bf16[256,2048]{1,0:T(8,128)(2,1)}, u32[]{:S(2)}, u32[]{:S(2)}) %collective-permute-start.1) | collective-permute-done | bytes 1048608 | tf_op jit(solution)/shard_map/ppermute | solution.py:23
  114.5 4.8 collective-permute-done
  121.3 4.1 gather_fusion
  125.5 18.6 %reshape.286 = bf16[4,320,2,4,4,64]{5,4,3,2,1,0:T(4,128)(2,1)} reshape(bf16[20,64,2048]{2,1,0:T(8,128)(2,1)} %gather_fusion) | data formatting | bytes 10485760 | tf_op jit(solution)/shard_map/reshape | solution.py:77
  144.1 17.9 %copy.19 = bf16[4,4,320,2,4,64]{2,5,4,1,3,0:T(8,128)(2,1)} copy(bf16[4,4,320,2,4,64]{5,4,0,3,2,1:T(4,128)(2,1)} %bitcast.175) | data formatting | bytes 10485760
  162.0 26.0 %while.28 = (s32[]{:T(128)}, bf16[4,4,64,4,64]{2,4,3,1,0:T(8,128)(2,1)S(1)}, bf16[4,4,320,2,4,64]{2,5,4,1,3,0:T(8,128)(2,1)}, bf16[4,4,64,4,64]{4,2,3,1,0:T(8,128)(2,1)}, pred[4,5]{1,0:T(4,128)(4,1)S(1)}, /*index=5*/s32[]{:T(128)}) while((s32[]{:T(128)}, bf16[4,4,64,4,64]{2,4,3,1,0:T(8,128)(2,1)S(1)}, ...), condition=%wide.region_4.5_spmd.clone, body=%wide.region_1.4_spmd.clone.sunk | while | flops 128845440 | bytes 5787497 | solution.py:100
  178.4 3.0 fusion.100
  194.6 57.7 %while.29 = (s32[]{:T(128)}, bf16[4,4,64,4,64]{2,4,3,1,0:T(8,128)(2,1)}, f32[4,4,320,2,4,64]{2,5,4,1,3,0:T(8,128)}, bf16[4,4,320,2,4,64]{2,5,4,1,3,0:T(8,128)(2,...) while((s32[]{:T(128)}, ...), condition=%wide.region_10.11_spmd.clone, body=%wide.region_6.10_spmd.clone.sunk | while | flops 214302016 | bytes 35685928 | solution.py:138
  252.3 23.2 %copy.24 = f32[4,320,2,4,4,64]{5,4,3,2,1,0:T(4,128)} copy(f32[4,320,2,4,4,64]{1,5,4,0,2,3:T(8,128)} %bitcast.177) | data formatting | bytes 20971520 | tf_op jit(solution)/shard_map/transpose | solution.py:140
  275.5 20.9 %reshape.306 = f32[20,64,2048]{2,1,0:T(8,128)} reshape(f32[4,320,2,4,4,64]{5,4,3,2,1,0:T(4,128)} %copy.24) | data formatting | bytes 20971520 | tf_op jit(solution)/shard_map/reshape | solution.py:140
  296.5 3.5 broadcast_in_dim.74
  300.0 22.1 %scatter_fusion = f32[12,64,2048]{2,1,0:T(8,128)} fusion(f32[12,64,2048]{2,1,0:T(8,128)} %broadcast_in_dim.74, s32[20]{0:T(128)S(1)} %fusion.68, f32[20,64,2048]{2,1,0:T(8,128)} %reshape.306), kind=kCustom, calls=%fused_computation.1 | custom fusion | flops 2621440 | bytes 31457360 | tf_op jit(solution)/shard_map/scatter-add | solution.py:142
  322.1 3.3 convert.19
  326.8 4.9 collective-permute-start.2
  334.5 9.7 %collective-permute-done.2 = bf16[4,64,2048]{2,1,0:T(8,128)(2,1)} collective-permute-done((bf16[4,64,2048]{2,1,0:T(8,128)(2,1)}, bf16[4,64,2048]{2,1,0:T(8,128)(2,1)}, u32[]{:S(2)}, u32[]{:S(2)}) %collective-permute-start.2) | collective-permute-done | bytes 1048608 | tf_op jit(solution)/shard_map/ppermute | solution.py:33
  347.0 4.6 convolution_convert_fusion.1
  351.7 89.4 %reduce-scatter.2.cloned.1.call-done = bf16[512,3072]{1,0:T(8,128)(2,1)} async-done(((bf16[1024,3072]{1,0:T(8,128)(2,1)}), bf16[512,3072]{1,0:T(8,128)(2,1)}) %reduce-scatter.2.cloned.1.call-update) | async-done | bytes 3145744 | tf_op jit(solution)/shard_map/reduce_scatter | solution.py:157
  441.2 4.7 multiply_reduce_fusion
  447.0 242.9 %all-gather.6.cloned.1.call-done = bf16[8192,3072]{1,0:T(8,128)(2,1)} async-done(((bf16[512,3072]{1,0:T(8,128)(2,1)}), bf16[8192,3072]{1,0:T(8,128)(2,1)}) %all-gather.6.cloned.1.call-update) | async-done | bytes 50331664 | tf_op jit(solution)/shard_map/all_gather | solution.py:165
  690.0 17.0 %reduce_sum.72 = bf16[512,3072]{1,0:T(8,128)(2,1)S(1)} reduce(bf16[16,512,3072]{2,1,0:T(8,128)(2,1)} %bitcast.174, bf16[]{:T(256)} %constant.153.clone.1), dimensions={0}, to_apply=%region_14.15 | reduce | flops 23592960 | bytes 53477376 | tf_op jit(solution)/shard_map/reduce_sum | solution.py:165
  706.9 3.5 convert_element_type.119
  (186 shorter events, 106.1 us)
Async XLA Ops:
  7.2 2.8 copy-start.10
  7.2 85.5 %all-gather.4.cloned.1.call-start = ((), (), s32[]{:S(2)}) async-start(), calls=%async_computation.1 | async-start | bytes 9437184 | tf_op jit(solution)/shard_map/all_gather | solution.py:64
  7.9 433.2 %reduce-scatter.2.cloned.1.call-start = ((), (), s32[]{:S(2)}) async-start(), calls=%async_computation.2 | async-start | bytes 9437184 | tf_op jit(solution)/shard_map/reduce_scatter | solution.py:157
  10.4 87.0 %copy-start = (f32[256,1024]{1,0:T(8,128)}, f32[256,1024]{1,0:T(8,128)S(1)}, u32[]{:S(2)}) copy-start(f32[256,1024]{1,0:T(8,128)S(1)} %get-tuple-element.197) | copy-start | bytes 3145732
  97.3 4.8 copy-start.11
  97.4 5.5 copy-start.13
  97.4 6.4 copy-start.15
  97.4 6.6 copy-start.17
  98.5 8.5 %copy-start.6 = (bf16[256,2048]{1,0:T(8,128)(2,1)}, bf16[256,2048]{1,0:T(8,128)(2,1)S(1)}, u32[]{:S(2)}) copy-start(bf16[256,2048]{1,0:T(8,128)(2,1)S(1)} %slice.82) | copy-start | bytes 3145732
  98.5 16.0 %collective-permute-start.1 = (bf16[256,2048]{1,0:T(8,128)(2,1)S(1)}, bf16[256,2048]{1,0:T(8,128)(2,1)}, u32[]{:S(2)}, u32[]{:S(2)}) collective-permute-start(bf16[256,2048]{1,0:T(8,128)(2,1)S(1)} %slice.82), channel_id=1, source_target_pairs={{2,0},{4,2},{6,4},{8,6},{10,8},{12,10},{14,12},{16,14},{18,16},{20... | collective-permute-start | bytes 3145736 | tf_op jit(solution)/shard_map/ppermute | solution.py:23
  102.2 17.1 %collective-permute-start = (bf16[256,2048]{1,0:T(8,128)(2,1)S(1)}, bf16[256,2048]{1,0:T(8,128)(2,1)}, u32[]{:S(2)}, u32[]{:S(2)}) collective-permute-start(bf16[256,2048]{1,0:T(8,128)(2,1)S(1)} %slice.82), channel_id=1, source_target_pairs={{0,2},{2,4},{4,6},{6,8},{8,10},{10,12},{12,14},{14,16},{16,18},{18... | collective-permute-start | bytes 3145736 | tf_op jit(solution)/shard_map/ppermute | solution.py:21
  144.1 17.9 %copy-start.2 = (bf16[4,4,64,4,64]{2,4,3,1,0:T(8,128)(2,1)S(1)}, bf16[4,4,64,4,64]{2,4,3,1,0:T(8,128)(2,1)}, u32[]{:S(2)}) copy-start(bf16[4,4,64,4,64]{2,4,3,1,0:T(8,128)(2,1)} %custom-call.2) | copy-start | bytes 1572868
  191.1 2.9 copy-start.1
  200.7 2.0 copy-start.8
  207.1 1.9 copy-start.5
  215.1 2.0 copy-start.8
  221.5 2.0 copy-start.5
  229.6 2.0 copy-start.8
  236.0 2.0 copy-start.5
  244.1 2.0 copy-start.8
  250.5 1.9 copy-start.5
  326.8 17.3 %collective-permute-start.2 = (bf16[4,64,2048]{2,1,0:T(8,128)(2,1)}, bf16[4,64,2048]{2,1,0:T(8,128)(2,1)}, u32[]{:S(2)}, u32[]{:S(2)}) collective-permute-start(bf16[4,64,2048]{2,1,0:T(8,128)(2,1)} %get-tuple-element.200), channel_id=1, source_target_pairs={{0,2},{2,4},{4,6},{6,8},{8,10},{10,12},{12,14},{14,16},{16,18},{18... | collective-permute-start | bytes 3145736 | tf_op jit(solution)/shard_map/ppermute | solution.py:33
  331.8 12.6 %collective-permute-start.3 = (bf16[4,64,2048]{2,1,0:T(8,128)(2,1)}, bf16[4,64,2048]{2,1,0:T(8,128)(2,1)}, u32[]{:S(2)}, u32[]{:S(2)}) collective-permute-start(bf16[4,64,2048]{2,1,0:T(8,128)(2,1)} %get-tuple-element.201), channel_id=1, source_target_pairs={{0,30},{2,0},{4,2},{6,4},{8,6},{10,8},{12,10},{14,12},{16,14},{18,... | collective-permute-start | bytes 3145736 | tf_op jit(solution)/shard_map/ppermute | solution.py:33
  351.7 338.3 %all-gather.6.cloned.1.call-start = ((), (), s32[]{:S(2)}) async-start(), calls=%async_computation.3 | async-start | bytes 53477376 | tf_op jit(solution)/shard_map/all_gather | solution.py:165
  (17 other events, 23.8 us)
Sparse Core Ops, SparseCore 0:
  9.6 83.0 all-gather.3
  351.8 89.2 reduce-scatter.1
  442.8 247.0 all-gather.5
